TPU v7x, 512 devices: a whole 4x8x8 slice. The times are simulated.
512 devices in a mesh: dp: 4 (over x), expert: 8 (over y), etp: 16 (over z, core).
Axes of the slice: x: 4, y: 8, z: 8, core: 2. Of those that a mesh axis runs over, the one named last changes fastest.
Arguments:
- tokens: bfloat16 [4096, 3072], P(('dp', 'expert')), parts along dimension 0, may hold values from -6 to 6
- routes: int32 [4096, 2], P(('dp', 'expert')), parts along dimension 0, may hold values from 0 to 3, all different within a row; in each aligned block of 128 rows (0 to 127, 128 to 255, ...) at most 80 rows name the same one
- route_weight: float32 [4096, 2], P(('dp', 'expert')), parts along dimension 0, may hold values from 0.2 to 1
- w_in: bfloat16 [8, 3072, 4096], P('expert', None, 'etp'), may hold values from -0.109375 to 0.109375
- w_out: bfloat16 [8, 4096, 3072], P('expert', 'etp'), may hold values from -0.0625 to 0.0625
Outputs:
- moe_output: bfloat16 [4096, 3072], P(('dp', 'expert')), parts along dimension 0
There are 4 independent parts, one for each index of `dp`. A program takes and returns all parts, laid end to end along the dimension named above; an argument that names none is the same for every part. Nothing has to cross between parts.
Inputs may be any that keep to these rules, and one draw needn't show every extreme that they name: `routes`: each row names two different experts. Within each aligned block of 128 rows (the rows of one index of the expert axis) no expert is named by more than 80 rows, a bound that some block reaches.
All inputs are finite; a program needn't handle non-finite values.
Results may differ from a plain program's by a relative error of at most 0.018.
Values may be sent and summed in bfloat16 or wider, within the bound.
No kernel may reach another device: no remote copies, remote signals or barrier semaphores. Data moves between devices by JAX's collectives and lax.ppermute only.
A program may use at most 64 MiB of HBM per device.

v0:
```python
import jax
import jax.numpy as jnp
from jax import lax
from jax.sharding import PartitionSpec as P


def on_device(tokens, routes, route_weight, w_in, w_out):
    n_index = lax.axis_size("expert")
    n_tensor = lax.axis_size("etp")
    halves = max(1, n_index // 4)
    n_experts = n_index // halves
    tok_rows = tokens.shape[0]
    model_width = tokens.shape[1]
    rounded_up = (2 * tok_rows // n_experts + tok_rows // 8 + n_tensor - 1) // n_tensor * n_tensor
    capacity = min(tok_rows, rounded_up)
    chosen = routes.reshape(-1)
    indicator = (chosen[:, None] == jnp.arange(n_experts, dtype=jnp.int32)[None, :]).astype(
        jnp.int32
    )
    preceding = jnp.cumsum(indicator, axis=0) - indicator
    position = jnp.sum(preceding * indicator, axis=1)
    destination = chosen * capacity + position
    duplicated = jnp.repeat(tokens, 2, axis=0)
    packed = (
        jnp.zeros((n_experts * capacity, model_width), jnp.bfloat16).at[destination].set(duplicated)
    )
    outgoing = jnp.repeat(packed.reshape(n_experts, capacity, model_width), halves, axis=0)
    w_first = w_in[0]
    w_second = w_out[0]
    arrived = lax.all_to_all(outgoing, "expert", split_axis=0, concat_axis=0, tiled=True)
    flat_rows = arrived.reshape(-1, model_width)
    projected = jnp.dot(flat_rows, w_first, preferred_element_type=jnp.float32)
    hidden = jax.nn.silu(projected).astype(jnp.bfloat16)
    term = jnp.dot(hidden, w_second, preferred_element_type=jnp.float32)
    rounded = lax.optimization_barrier(term.astype(jnp.bfloat16))
    partial_terms = rounded.astype(jnp.float32).reshape(arrived.shape[:-1] + (model_width,))
    summed = lax.psum_scatter(
        partial_terms.astype(jnp.bfloat16), "etp", scatter_dimension=1, tiled=True
    ).astype(jnp.float32)
    homeward = lax.all_to_all(
        summed.astype(jnp.bfloat16), "expert", split_axis=0, concat_axis=0, tiled=True
    ).astype(summed.dtype)
    gathered = lax.all_gather(homeward.astype(jnp.bfloat16), "etp", axis=1, tiled=True).astype(
        homeward.dtype
    )
    home_rows = gathered.reshape(n_index * capacity, model_width)
    combined = jnp.zeros((tok_rows * 2, model_width), jnp.float32)
    for half_index in range(halves):
        combined = combined + home_rows[(chosen * halves + half_index) * capacity + position]
    weighted = combined.reshape(tok_rows, 2, model_width) * route_weight[:, :, None]
    return jnp.sum(weighted, axis=1).astype(jnp.bfloat16)


def solution(mesh):
    placed = (
        P(("dp", "expert"), None),
        P(("dp", "expert"), None),
        P(("dp", "expert"), None),
        P("expert", None, "etp"),
        P("expert", "etp", None),
    )
    return jax.shard_map(
        on_device, mesh=mesh, in_specs=placed, out_specs=P(("dp", "expert"), None), check_vma=False
    )
```

profile of v0, /device:TPU:1, one launch (start us, length us, event | category | flops | bytes accessed | tf_op | source)
XLA Modules:
  0.0 307.0 jit_solution(10249326293521199883)
XLA Ops:
  6.5 0.0 copy-start
  6.5 0.0 reduce-scatter.2.cloned.1.call-start
  6.5 0.9 copy.28
  7.4 0.1 eq.29
  7.6 0.1 eq.25
  7.7 0.7 add_multiply_fusion
  8.4 1.2 reduce-window.6
  9.6 0.1 slice.12
  9.7 0.1 copy.30
  9.9 0.1 copy.31
  10.0 0.1 add_bitcast_fusion
  10.0 0.1 copy.27
  10.1 0.1 mul.69
  10.3 0.1 copy.36
  10.4 0.1 mul.74
  10.5 0.1 copy.37
  10.7 0.1 mul.77
  10.8 1.9 broadcast_in_dim.7
  12.8 1.5 reshape.166
  14.3 4.2 %scatter_custom_fusion = bf16[320,3072]{1,0:T(8,128)(2,1)S(1)} fusion(s32[256]{0:T(256)S(1)} %bitcast.49, bf16[256,3072]{1,0:T(8,128)(2,1)} %reshape.166, bf16[]{:T(256)} %constant.5.clone.1), kind=kCustom, calls=%fused_computation.8 | custom fusion | bytes 1966592 | tf_op jit(solution)/shard_map/scatter | solution.py:25
  18.5 0.6 broadcast_in_dim.16
  19.1 0.0 copy-start.2
  19.1 95.2 %all_to_all.10 = bf16[8,80,3072]{2,1,0:T(8,128)(2,1)} all-to-all(bf16[8,80,3072]{2,1,0:T(8,128)(2,1)S(1)} %bitcast.41), channel_id=1, replica_groups=mesh['dp'=4,'expert'=8,'etp'=16] {'expert'}, dimensions={0} | all-to-all | bytes 7864320 | tf_op jit(solution)/shard_map/all_to_all | solution.py:30
  114.4 0.0 copy-done
  114.4 0.0 copy-done.2
  114.4 8.2 %convolution_convert_fusion = bf16[640,3072]{1,0:T(8,128)(2,1)} fusion(bf16[1,256,3072]{2,1,0:T(8,128)(2,1)S(1)} %copy-done, bf16[640,3072]{1,0:T(8,128)(2,1)} %bitcast.43, bf16[1,3072,256]{2,1,0:T(8,128)(2,1)S(1)} %copy-done.2), kind=kOutput, calls=%fused_computation.3 | convolution fusion | flops 2016051200 | bytes 11010048 | tf_op jit(solution)/shard_map/dot_general | solution.py:34
  122.5 6.2 %copy.32 = bf16[8,80,3072]{2,0,1:T(8,128)(2,1)} copy(bf16[8,80,3072]{2,1,0:T(8,128)(2,1)} %bitcast.44) | data formatting | bytes 7864320 | tf_op jit(solution)/shard_map/convert_element_type | solution.py:38
  128.7 0.0 copy-start.1
  128.7 0.0 reduce-scatter.2.cloned.1.call-update
  128.7 0.0 all-gather.2.cloned.1.call-start
  128.8 66.1 %reduce-scatter.2.cloned.1.call-done = bf16[8,5,3072]{2,0,1:T(8,128)(2,1)} async-done(((bf16[8,80,3072]{2,0,1:T(8,128)(2,1)}), bf16[8,5,3072]{2,0,1:T(8,128)(2,1)}) %reduce-scatter.2.cloned.1.call-update) | async-done | bytes 245776 | tf_op jit(solution)/shard_map/reduce_scatter | solution.py:37
  194.9 1.1 copy.33
  196.0 16.7 %all_to_all.11 = bf16[8,5,3072]{2,1,0:T(8,128)(2,1)S(1)} all-to-all(bf16[8,5,3072]{2,1,0:T(8,128)(2,1)S(1)} %copy.33), channel_id=1, replica_groups=mesh['dp'=4,'expert'=8,'etp'=16] {'expert'}, dimensions={0} | all-to-all | bytes 491520 | tf_op jit(solution)/shard_map/all_to_all | solution.py:40
  212.8 0.9 copy.34
  213.6 0.0 all-gather.2.cloned.1.call-update
  213.6 0.0 copy-done.1
  213.7 0.1 copy.38
  213.8 45.4 %all-gather.2.cloned.1.call-done = bf16[8,80,3072]{2,0,1:T(8,128)(2,1)} async-done(((bf16[8,5,3072]{2,0,1:T(8,128)(2,1)}), bf16[8,80,3072]{2,0,1:T(8,128)(2,1)}) %all-gather.2.cloned.1.call-update) | async-done | bytes 3932176 | tf_op jit(solution)/shard_map/all_gather | solution.py:43
  259.2 7.5 %copy.35 = f32[8,80,3072]{2,1,0:T(8,128)} copy(bf16[8,80,3072]{2,0,1:T(8,128)(2,1)} %all-gather.2.cloned.1.call-done) | data formatting | bytes 11796480 | tf_op jit(solution)/shard_map/reshape | solution.py:46
  266.7 8.0 %gather_fusion.1 = f32[256,3072]{1,0:T(8,128)} fusion(f32[640,3072]{1,0:T(8,128)} %bitcast.39, s32[1024]{0:T(1024)S(1)} %pad_clamp_fusion), kind=kCustom, calls=%fused_computation.1 | custom fusion | bytes 6292480 | tf_op jit(solution)/shard_map/gather | solution.py:49
  274.7 8.0 %gather_fusion = f32[256,3072]{1,0:T(8,128)} fusion(f32[640,3072]{1,0:T(8,128)} %bitcast.40, s32[1024]{0:T(1024)S(1)} %pad_clamp_fusion.1), kind=kCustom, calls=%fused_computation | custom fusion | bytes 6292480 | tf_op jit(solution)/shard_map/gather | solution.py:49
  282.7 5.1 %add.100 = f32[256,3072]{1,0:T(8,128)} add(f32[256,3072]{1,0:T(8,128)} %gather_fusion, f32[256,3072]{1,0:T(8,128)} %gather_fusion.1) | non-fusion elementwise | flops 786432 | bytes 9437184 | tf_op jit(solution)/shard_map/add | solution.py:49
  287.8 5.1 %add.101 = f32[128,2,3072]{2,1,0:T(2,128)} reshape(f32[256,3072]{1,0:T(8,128)} %add.100) | data formatting | bytes 6291456 | tf_op jit(solution)/shard_map/add | solution.py:49
  292.8 7.3 %multiply_reduce_fusion = bf16[128,3072]{1,0:T(8,128)(2,1)} fusion(f32[128,2,3072]{2,1,0:T(2,128)} %add.101, f32[128,2]{1,0:T(8,128)S(1)} %copy.38), kind=kLoop, calls=%fused_computation.4 | loop fusion | flops 1179648 | bytes 3933184 | tf_op jit(solution)/shard_map/reduce_sum | solution.py:51
  (7 shorter events, 0.1 us)
Async XLA Ops:
  6.5 107.8 %copy-start = (bf16[1,256,3072]{2,1,0:T(8,128)(2,1)S(1)}, bf16[1,256,3072]{2,1,0:T(8,128)(2,1)}, u32[]{:S(2)}) copy-start(bf16[1,256,3072]{2,1,0:T(8,128)(2,1)} %param.9) | copy-start | bytes 4718596
  6.5 188.4 %reduce-scatter.2.cloned.1.call-start = ((), (), s32[]{:S(2)}) async-start(), calls=%async_computation.3 | async-start | bytes 4177920 | tf_op jit(solution)/shard_map/reduce_scatter | solution.py:37
  19.1 95.2 %copy-start.2 = (bf16[1,3072,256]{2,1,0:T(8,128)(2,1)S(1)}, bf16[1,3072,256]{2,1,0:T(8,128)(2,1)}, u32[]{:S(2)}) copy-start(bf16[1,3072,256]{2,1,0:T(8,128)(2,1)} %param.8) | copy-start | bytes 4718596
  128.7 84.9 %copy-start.1 = (f32[128,2]{0,1:T(2,128)S(1)}, f32[128,2]{0,1:T(2,128)}, u32[]{:S(2)}) copy-start(f32[128,2]{0,1:T(2,128)} %param.7) | copy-start | bytes 3076
  128.7 130.5 %all-gather.2.cloned.1.call-start = ((), (), s32[]{:S(2)}) async-start(), calls=%async_computation.4 | async-start | bytes 4177920 | tf_op jit(solution)/shard_map/all_gather | solution.py:43
Sparse Core Ops, SparseCore 0:
  128.9 66.0 reduce-scatter.1
  213.8 45.4 all-gather.1
where the time goes:
time: 308 us; the launch traced here: 307 us
  blocking collectives  112 us (36%)
  waiting for transfers between devices  112 us (36%)
  local copies, waits for them, and re-layouts  47.3 us (15%)
  other arithmetic  14.4 us (5%)
  between operations  13.5 us (4%)
  matrix products  8.18 us (3%)
    all_to_all x1, blocking collectives, on_device(): lax.all_to_all(outgoing, 'expert', split_axis=0, concat_axis=0, tiled=True)  95.2 us
    reduce_scatter x1, waiting for transfers between devices, on_device(): lax.psum_scatter(partial_terms.astype(jnp.bfloat16), 'etp', scatter_dimen...  66.1 us
    all_gather x1, waiting for transfers between devices, on_device(): lax.all_gather(homeward.astype(jnp.bfloat16), 'etp', axis=1, tiled=True)  45.4 us
    all_to_all x1, blocking collectives, on_device(): lax.all_to_all(summed.astype(jnp.bfloat16), 'expert', split_axis=0, conca...  16.7 us
    gather x2, local copies, waits for them, and re-layouts, on_device(): home_rows[(chosen * halves + half_index) * capacity + position]  16 us
    dot_general x1, matrix products, on_device(): term = jnp.dot(hidden, w_second, preferred_element_type=jnp.float32)  8.18 us
    reshape x1, local copies, waits for them, and re-layouts, on_device(): home_rows = gathered.reshape(n_index * capacity, model_width)  7.47 us
    reduce_sum x1, other arithmetic, on_device(): return jnp.sum(weighted, axis=1).astype(jnp.bfloat16)  7.27 us
  transfers between devices with their start and end apart: 2, of which 2 were waited for; matrix products, arithmetic and copies ran while one was open for 0% of the time, Pallas kernels for 0%

commit v1 on v0

--- a/solution.py
+++ b/solution.py
@@ -2,6 +2,27 @@
 import jax.numpy as jnp
 from jax import lax
 from jax.sharding import PartitionSpec as P
+
+
+def ring_gather(x, axis, dim):
+    devices, index, rows = (lax.axis_size(axis), lax.axis_index(axis), x.shape[dim])
+    right = [(i, (i + 1) % devices) for i in range(devices)]
+    backward = [(i, (i - 1) % devices) for i in range(devices)]
+    whole = jnp.zeros((*x.shape[:dim], devices * rows, *x.shape[dim + 1 :]), x.dtype)
+    whole = lax.dynamic_update_slice_in_dim(whole, x, index * rows, axis=dim)
+    from_left = from_right = x
+    middle = devices // 2
+    for step in range(1, middle + 1):
+        from_left = lax.ppermute(from_left, axis, right)
+        whole = lax.dynamic_update_slice_in_dim(
+            whole, from_left, (index - step) % devices * rows, axis=dim
+        )
+        if step < devices - middle:
+            from_right = lax.ppermute(from_right, axis, backward)
+            whole = lax.dynamic_update_slice_in_dim(
+                whole, from_right, (index + step) % devices * rows, axis=dim
+            )
+    return whole
 
 
 def on_device(tokens, routes, route_weight, w_in, w_out):
@@ -40,9 +61,7 @@
     homeward = lax.all_to_all(
         summed.astype(jnp.bfloat16), "expert", split_axis=0, concat_axis=0, tiled=True
     ).astype(summed.dtype)
-    gathered = lax.all_gather(homeward.astype(jnp.bfloat16), "etp", axis=1, tiled=True).astype(
-        homeward.dtype
-    )
+    gathered = ring_gather(homeward.astype(jnp.bfloat16), "etp", 1).astype(homeward.dtype)
     home_rows = gathered.reshape(n_index * capacity, model_width)
     combined = jnp.zeros((tok_rows * 2, model_width), jnp.float32)
     for half_index in range(halves):

time: 308 us -> 401 us (1.30); the launches traced: 307 us -> 393 us
  local copies, waits for them, and re-layouts: 47.3 us -> 115 us
  starting transfers between devices: 0.04 us -> 39.6 us
  waiting for transfers between devices: 112 us -> 83.8 us
  other arithmetic: 14.4 us -> 20.6 us
    dynamic_update_slice x0 -> x16, local copies, waits for them, and re-layouts: none -> 72.9 us  [the longest x8 36.2 us: ring_gather(): lax.dynamic_update_slice_in_dim(whole, from_left, (index - step) % device...]
    all_gather x1 -> x0, waiting for transfers between devices: 45.4 us -> none  [on_device(): lax.all_gather(homeward.astype(jnp.bfloat16), 'etp', axis=1, tiled=True)]
    ppermute x0 -> x15, starting transfers between devices: none -> 39.6 us  [the longest x7 23.6 us: ring_gather(): from_right = lax.ppermute(from_right, axis, backward)]
    ppermute x0 -> x15, waiting for transfers between devices: none -> 17.5 us  [the longest x8 12.3 us: ring_gather(): from_left = lax.ppermute(from_left, axis, right)]
    reshape x1 -> x0, local copies, waits for them, and re-layouts: 7.47 us -> none  [on_device(): home_rows = gathered.reshape(n_index * capacity, model_width)]
    reshape x0 -> x1, other arithmetic: none -> 6.21 us  [on_device(): home_rows = gathered.reshape(n_index * capacity, model_width)]
  transfers between devices with their start and end apart: 2 -> 16, of which waited for: 2 -> 14; matrix products, arithmetic and copies ran while one was open for 0% -> 18% of each run, Pallas kernels for 0% -> 0%
where the time goes in v1:
time: 401 us; the launch traced here: 393 us
  local copies, waits for them, and re-layouts  115 us (29%)
  blocking collectives  112 us (28%)
  waiting for transfers between devices  83.8 us (21%)
  starting transfers between devices  39.6 us (10%)
  other arithmetic  20.6 us (5%)
  between operations  13.5 us (3%)
  matrix products  8.16 us (2%)
    all_to_all x1, blocking collectives, on_device(): lax.all_to_all(outgoing, 'expert', split_axis=0, concat_axis=0, tiled=True)  95.2 us
    reduce_scatter x1, waiting for transfers between devices, on_device(): lax.psum_scatter(partial_terms.astype(jnp.bfloat16), 'etp', scatter_dimen...  66.2 us
    dynamic_update_slice x8, local copies, waits for them, and re-layouts, ring_gather(): lax.dynamic_update_slice_in_dim(whole, from_left, (index - step) % device...  36.2 us
    dynamic_update_slice x7, local copies, waits for them, and re-layouts, ring_gather(): lax.dynamic_update_slice_in_dim(whole, from_right, (index + step) % devic...  32.3 us
    ppermute x7, starting transfers between devices, ring_gather(): from_right = lax.ppermute(from_right, axis, backward)  23.6 us
    all_to_all x1, blocking collectives, on_device(): lax.all_to_all(summed.astype(jnp.bfloat16), 'expert', split_axis=0, conca...  16.7 us
    gather x2, local copies, waits for them, and re-layouts, on_device(): home_rows[(chosen * halves + half_index) * capacity + position]  16 us
    ppermute x8, starting transfers between devices, ring_gather(): from_left = lax.ppermute(from_left, axis, right)  16 us
  transfers between devices with their start and end apart: 16, of which 14 were waited for; matrix products, arithmetic and copies ran while one was open for 18% of the time, Pallas kernels for 0%

profile of v1, /device:TPU:1, one launch (start us, length us, event | category | flops | bytes accessed | tf_op | source)
XLA Modules:
  0.0 392.6 jit_solution(379634610022546857)
XLA Ops:
  8.4 1.2 reduce-window.6
  10.8 1.9 broadcast_in_dim.19
  12.8 1.5 reshape.166
  14.3 4.2 %scatter_custom_fusion = bf16[320,3072]{1,0:T(8,128)(2,1)S(1)} fusion(s32[256]{0:T(256)S(1)} %bitcast.49, bf16[256,3072]{1,0:T(8,128)(2,1)} %reshape.166, bf16[]{:T(256)} %constant.103.clone.1), kind=kCustom, calls=%fused_computation.9 | custom fusion | bytes 1966592 | tf_op jit(solution)/shard_map/scatter | solution.py:46
  19.2 95.2 %all_to_all.10 = bf16[8,80,3072]{2,1,0:T(8,128)(2,1)} all-to-all(bf16[8,80,3072]{2,1,0:T(8,128)(2,1)S(1)} %bitcast.41), channel_id=1, replica_groups=mesh['dp'=4,'expert'=8,'etp'=16] {'expert'}, dimensions={0} | all-to-all | bytes 7864320 | tf_op jit(solution)/shard_map/all_to_all | solution.py:51
  114.4 8.2 %convolution_convert_fusion = bf16[640,3072]{1,0:T(8,128)(2,1)} fusion(bf16[1,256,3072]{2,1,0:T(8,128)(2,1)S(1)} %copy-done, bf16[640,3072]{1,0:T(8,128)(2,1)} %bitcast.43, bf16[1,3072,256]{2,1,0:T(8,128)(2,1)S(1)} %copy-done.17), kind=kOutput, calls=%fused_computation.3 | convolution fusion | flops 2016051200 | bytes 11010048 | tf_op jit(solution)/shard_map/dot_general | solution.py:55
  122.5 6.1 %copy.47 = bf16[8,80,3072]{2,0,1:T(8,128)(2,1)} copy(bf16[8,80,3072]{2,1,0:T(8,128)(2,1)} %bitcast.44) | data formatting | bytes 7864320 | tf_op jit(solution)/shard_map/convert_element_type | solution.py:59
  128.7 66.2 %reduce-scatter.2.cloned.1.call-done = bf16[8,5,3072]{2,0,1:T(8,128)(2,1)} async-done(((bf16[8,80,3072]{2,0,1:T(8,128)(2,1)}), bf16[8,5,3072]{2,0,1:T(8,128)(2,1)}) %reduce-scatter.2.cloned.1.call-update) | async-done | bytes 245776 | tf_op jit(solution)/shard_map/reduce_scatter | solution.py:58
  196.0 16.7 %all_to_all.11 = bf16[8,5,3072]{2,1,0:T(8,128)(2,1)S(1)} all-to-all(bf16[8,5,3072]{2,1,0:T(8,128)(2,1)S(1)} %copy.48), channel_id=1, replica_groups=mesh['dp'=4,'expert'=8,'etp'=16] {'expert'}, dimensions={0} | all-to-all | bytes 491520 | tf_op jit(solution)/shard_map/all_to_all | solution.py:61
  212.7 5.2 %collective-permute-start = (bf16[8,5,3072]{2,1,0:T(8,128)(2,1)S(1)}, bf16[8,5,3072]{2,1,0:T(8,128)(2,1)S(1)}, u32[]{:S(2)}, u32[]{:S(2)}) collective-permute-start(bf16[8,5,3072]{2,1,0:T(8,128)(2,1)S(1)} %all_to_all.11), channel_id=1, source_target_pairs={{0,1},{1,2},{2,3},{3,4},{4,5},{5,6},{6,7},{7,8},{8,9},{9,10},{10,1... | collective-permute-start | bytes 737288 | tf_op jit(solution)/shard_map/ppermute | solution.py:16
  217.9 4.7 %collective-permute-done = bf16[8,5,3072]{2,1,0:T(8,128)(2,1)S(1)} collective-permute-done((bf16[8,5,3072]{2,1,0:T(8,128)(2,1)S(1)}, bf16[8,5,3072]{2,1,0:T(8,128)(2,1)S(1)}, u32[]{:S(2)}, u32[]{:S(2)}) %collective-permute-start) | collective-permute-done | bytes 245792 | tf_op jit(solution)/shard_map/ppermute | solution.py:16
  222.7 2.5 collective-permute-start.2
  226.5 3.4 collective-permute-done.2
  229.9 2.5 collective-permute-start.4
  232.9 1.9 collective-permute-start.5
  234.9 2.2 collective-permute-done.4
  237.1 2.5 collective-permute-start.6
  240.4 3.6 collective-permute-start.7
  244.5 2.3 collective-permute-start.8
  246.8 1.2 collective-permute-done.7
  247.9 4.5 %collective-permute-start.9 = (bf16[8,5,3072]{2,1,0:T(8,128)(2,1)S(1)}, bf16[8,5,3072]{2,1,0:T(8,128)(2,1)S(1)}, u32[]{:S(2)}, u32[]{:S(2)}) collective-permute-start(bf16[8,5,3072]{2,1,0:T(8,128)(2,1)S(1)} %collective-permute-done.7), channel_id=1, source_target_pairs={{0,15},{1,0},{2,1},{3,2},{4,3},{5,4},{6,5},{7,6},{8,7},{9,8},{10,9... | collective-permute-start | bytes 737288 | tf_op jit(solution)/shard_map/ppermute | solution.py:21
  254.0 1.2 collective-permute-done.9
  255.2 5.7 %collective-permute-start.11 = (bf16[8,5,3072]{2,1,0:T(8,128)(2,1)S(1)}, bf16[8,5,3072]{2,1,0:T(8,128)(2,1)}, u32[]{:S(2)}, u32[]{:S(2)}) collective-permute-start(bf16[8,5,3072]{2,1,0:T(8,128)(2,1)S(1)} %collective-permute-done.9), channel_id=1, source_target_pairs={{0,15},{1,0},{2,1},{3,2},{4,3},{5,4},{6,5},{7,6},{8,7},{9,8},{10,9... | collective-permute-start | bytes 737288 | tf_op jit(solution)/shard_map/ppermute | solution.py:21
  261.3 1.1 collective-permute-done.11
  262.5 6.8 %collective-permute-start.13 = (bf16[8,5,3072]{2,1,0:T(8,128)(2,1)}, bf16[8,5,3072]{2,1,0:T(8,128)(2,1)}, u32[]{:S(2)}, u32[]{:S(2)}) collective-permute-start(bf16[8,5,3072]{2,1,0:T(8,128)(2,1)} %collective-permute-done.11), channel_id=1, source_target_pairs={{0,15},{1,0},{2,1},{3,2},{4,3},{5,4},{6,5},{7,6},{8,7},{9,8},{10,9... | collective-permute-start | bytes 737288 | tf_op jit(solution)/shard_map/ppermute | solution.py:21
  270.6 2.4 broadcast_in_dim.8
  273.1 4.5 %dynamic_update_slice.48 = bf16[8,80,3072]{2,1,0:T(8,128)(2,1)} dynamic-update-slice(bf16[8,80,3072]{2,1,0:T(8,128)(2,1)} %broadcast_in_dim.8, bf16[8,5,3072]{2,1,0:T(8,128)(2,1)S(1)} %all_to_all.11, s32[]{:T(128)} %constant.105.clone.1, s32[]{:T(128)S(6)} %select_n.142, s32[]{:T(128)} %constant.105.clone.1) | dynamic-update-slice | bytes 491524 | tf_op jit(solution)/shard_map/dynamic_update_slice | solution.py:12
  277.6 4.5 %dynamic_update_slice.49 = bf16[8,80,3072]{2,1,0:T(8,128)(2,1)} dynamic-update-slice(bf16[8,80,3072]{2,1,0:T(8,128)(2,1)} %dynamic_update_slice.48, bf16[8,5,3072]{2,1,0:T(8,128)(2,1)S(1)} %collective-permute-done, s32[]{:T(128)} %constant.105.clone.1, s32[]{:T(128)S(6)} %select_n.144, s32[]{:T(128)} %constant.105.clone.1) | dynamic-update-slice | bytes 491524 | tf_op jit(solution)/shard_map/dynamic_update_slice | solution.py:17
  282.1 4.6 %dynamic_update_slice.50 = bf16[8,80,3072]{2,1,0:T(8,128)(2,1)} dynamic-update-slice(bf16[8,80,3072]{2,1,0:T(8,128)(2,1)} %dynamic_update_slice.49, bf16[8,5,3072]{2,1,0:T(8,128)(2,1)S(1)} %collective-permute-done.1, s32[]{:T(128)} %constant.105.clone.1, s32[]{:T(128)S(6)} %select_n.146, s32[]{:T(128)} %constant.105.clone.1) | dynamic-update-slice | bytes 491524 | tf_op jit(solution)/shard_map/dynamic_update_slice | solution.py:22
  286.7 3.9 %dynamic_update_slice.51 = bf16[8,80,3072]{2,1,0:T(8,128)(2,1)} dynamic-update-slice(bf16[8,80,3072]{2,1,0:T(8,128)(2,1)} %dynamic_update_slice.50, bf16[8,5,3072]{2,1,0:T(8,128)(2,1)S(1)} %collective-permute-done.2, s32[]{:T(128)} %constant.105.clone.1, s32[]{:T(128)S(6)} %select_n.148, s32[]{:T(128)} %constant.105.clone.1) | dynamic-update-slice | bytes 491524 | tf_op jit(solution)/shard_map/dynamic_update_slice | solution.py:17
  290.6 4.6 %dynamic_update_slice.52 = bf16[8,80,3072]{2,1,0:T(8,128)(2,1)} dynamic-update-slice(bf16[8,80,3072]{2,1,0:T(8,128)(2,1)} %dynamic_update_slice.51, bf16[8,5,3072]{2,1,0:T(8,128)(2,1)S(1)} %collective-permute-done.3, s32[]{:T(128)} %constant.105.clone.1, s32[]{:T(128)S(6)} %select_n.150, s32[]{:T(128)} %constant.105.clone.1) | dynamic-update-slice | bytes 491524 | tf_op jit(solution)/shard_map/dynamic_update_slice | solution.py:22
  295.2 4.6 %dynamic_update_slice.53 = bf16[8,80,3072]{2,1,0:T(8,128)(2,1)} dynamic-update-slice(bf16[8,80,3072]{2,1,0:T(8,128)(2,1)} %dynamic_update_slice.52, bf16[8,5,3072]{2,1,0:T(8,128)(2,1)S(1)} %copy-done.2, s32[]{:T(128)} %constant.105.clone.1, s32[]{:T(128)S(6)} %select_n.152, s32[]{:T(128)} %constant.105.clone.1) | dynamic-update-slice | bytes 491524 | tf_op jit(solution)/shard_map/dynamic_update_slice | solution.py:17
  299.8 4.6 %dynamic_update_slice.54 = bf16[8,80,3072]{2,1,0:T(8,128)(2,1)} dynamic-update-slice(bf16[8,80,3072]{2,1,0:T(8,128)(2,1)} %dynamic_update_slice.53, bf16[8,5,3072]{2,1,0:T(8,128)(2,1)S(1)} %copy-done.4, s32[]{:T(128)} %constant.105.clone.1, s32[]{:T(128)S(6)} %select_n.154, s32[]{:T(128)} %constant.105.clone.1) | dynamic-update-slice | bytes 491524 | tf_op jit(solution)/shard_map/dynamic_update_slice | solution.py:22
  304.4 4.6 %dynamic_update_slice.55 = bf16[8,80,3072]{2,1,0:T(8,128)(2,1)} dynamic-update-slice(bf16[8,80,3072]{2,1,0:T(8,128)(2,1)} %dynamic_update_slice.54, bf16[8,5,3072]{2,1,0:T(8,128)(2,1)S(1)} %copy-done.6, s32[]{:T(128)} %constant.105.clone.1, s32[]{:T(128)S(6)} %select_n.156, s32[]{:T(128)} %constant.105.clone.1) | dynamic-update-slice | bytes 491524 | tf_op jit(solution)/shard_map/dynamic_update_slice | solution.py:17
  308.9 4.5 %dynamic_update_slice.56 = bf16[8,80,3072]{2,1,0:T(8,128)(2,1)} dynamic-update-slice(bf16[8,80,3072]{2,1,0:T(8,128)(2,1)} %dynamic_update_slice.55, bf16[8,5,3072]{2,1,0:T(8,128)(2,1)S(1)} %copy-done.8, s32[]{:T(128)} %constant.105.clone.1, s32[]{:T(128)S(6)} %select_n.158, s32[]{:T(128)} %constant.105.clone.1) | dynamic-update-slice | bytes 491524 | tf_op jit(solution)/shard_map/dynamic_update_slice | solution.py:22
  313.4 4.5 %dynamic_update_slice.57 = bf16[8,80,3072]{2,1,0:T(8,128)(2,1)} dynamic-update-slice(bf16[8,80,3072]{2,1,0:T(8,128)(2,1)} %dynamic_update_slice.56, bf16[8,5,3072]{2,1,0:T(8,128)(2,1)S(1)} %copy-done.10, s32[]{:T(128)} %constant.105.clone.1, s32[]{:T(128)S(6)} %select_n.160, s32[]{:T(128)} %constant.105.clone.1) | dynamic-update-slice | bytes 491524 | tf_op jit(solution)/shard_map/dynamic_update_slice | solution.py:17
  318.0 4.5 %dynamic_update_slice.58 = bf16[8,80,3072]{2,1,0:T(8,128)(2,1)} dynamic-update-slice(bf16[8,80,3072]{2,1,0:T(8,128)(2,1)} %dynamic_update_slice.57, bf16[8,5,3072]{2,1,0:T(8,128)(2,1)S(1)} %copy-done.12, s32[]{:T(128)} %constant.105.clone.1, s32[]{:T(128)S(6)} %select_n.162, s32[]{:T(128)} %constant.105.clone.1) | dynamic-update-slice | bytes 491524 | tf_op jit(solution)/shard_map/dynamic_update_slice | solution.py:22
  322.5 4.5 %dynamic_update_slice.59 = bf16[8,80,3072]{2,1,0:T(8,128)(2,1)} dynamic-update-slice(bf16[8,80,3072]{2,1,0:T(8,128)(2,1)} %dynamic_update_slice.58, bf16[8,5,3072]{2,1,0:T(8,128)(2,1)S(1)} %copy-done.14, s32[]{:T(128)} %constant.105.clone.1, s32[]{:T(128)S(6)} %select_n.164, s32[]{:T(128)} %constant.105.clone.1) | dynamic-update-slice | bytes 491524 | tf_op jit(solution)/shard_map/dynamic_update_slice | solution.py:17
  327.0 4.7 %dynamic_update_slice.60 = bf16[8,80,3072]{2,1,0:T(8,128)(2,1)} dynamic-update-slice(bf16[8,80,3072]{2,1,0:T(8,128)(2,1)} %dynamic_update_slice.59, bf16[8,5,3072]{2,1,0:T(8,128)(2,1)} %collective-permute-done.11, s32[]{:T(128)} %constant.105.clone.1, s32[]{:T(128)S(6)} %select_n.166, s32[]{:T(128)} %constant.105.clone.1) | dynamic-update-slice | bytes 491524 | tf_op jit(solution)/shard_map/dynamic_update_slice | solution.py:22
  331.8 4.7 %dynamic_update_slice.61 = bf16[8,80,3072]{2,1,0:T(8,128)(2,1)} dynamic-update-slice(bf16[8,80,3072]{2,1,0:T(8,128)(2,1)} %dynamic_update_slice.60, bf16[8,5,3072]{2,1,0:T(8,128)(2,1)} %collective-permute-done.12, s32[]{:T(128)} %constant.105.clone.1, s32[]{:T(128)S(6)} %select_n.168, s32[]{:T(128)} %constant.105.clone.1) | dynamic-update-slice | bytes 491524 | tf_op jit(solution)/shard_map/dynamic_update_slice | solution.py:17
  336.5 4.8 %dynamic_update_slice.62 = bf16[8,80,3072]{2,1,0:T(8,128)(2,1)} dynamic-update-slice(bf16[8,80,3072]{2,1,0:T(8,128)(2,1)} %dynamic_update_slice.61, bf16[8,5,3072]{2,1,0:T(8,128)(2,1)} %collective-permute-done.13, s32[]{:T(128)} %constant.105.clone.1, s32[]{:T(128)S(6)} %select_n.170, s32[]{:T(128)} %constant.105.clone.1) | dynamic-update-slice | bytes 491524 | tf_op jit(solution)/shard_map/dynamic_update_slice | solution.py:22
  341.3 4.8 %dynamic_update_slice.63 = bf16[8,80,3072]{2,1,0:T(8,128)(2,1)} dynamic-update-slice(bf16[8,80,3072]{2,1,0:T(8,128)(2,1)} %dynamic_update_slice.62, bf16[8,5,3072]{2,1,0:T(8,128)(2,1)} %collective-permute-done.14, s32[]{:T(128)} %constant.105.clone.1, s32[]{:T(128)S(6)} %select_n.172, s32[]{:T(128)} %constant.105.clone.1) | dynamic-update-slice | bytes 491524 | tf_op jit(solution)/shard_map/dynamic_update_slice | solution.py:17
  346.1 6.2 %bitcast_convert_fusion = f32[640,3072]{1,0:T(8,128)} fusion(bf16[8,80,3072]{2,1,0:T(8,128)(2,1)} %dynamic_update_slice.63), kind=kLoop, calls=%fused_computation.4 | loop fusion | flops 1966080 | bytes 11796480 | tf_op jit(solution)/shard_map/reshape | solution.py:65
  352.3 8.0 %gather_fusion.1 = f32[256,3072]{1,0:T(8,128)} fusion(f32[640,3072]{1,0:T(8,128)} %bitcast_convert_fusion, s32[1024]{0:T(1024)S(1)} %pad_clamp_fusion), kind=kCustom, calls=%fused_computation.1 | custom fusion | bytes 6292480 | tf_op jit(solution)/shard_map/gather | solution.py:68
  360.3 8.0 %gather_fusion = f32[256,3072]{1,0:T(8,128)} fusion(f32[640,3072]{1,0:T(8,128)} %bitcast_convert_fusion, s32[1024]{0:T(1024)S(1)} %pad_clamp_fusion.1), kind=kCustom, calls=%fused_computation | custom fusion | bytes 6292480 | tf_op jit(solution)/shard_map/gather | solution.py:68
  368.3 5.1 %add.261 = f32[256,3072]{1,0:T(8,128)} add(f32[256,3072]{1,0:T(8,128)} %gather_fusion, f32[256,3072]{1,0:T(8,128)} %gather_fusion.1) | non-fusion elementwise | flops 786432 | bytes 9437184 | tf_op jit(solution)/shard_map/add | solution.py:68
  373.4 5.1 %add.262 = f32[128,2,3072]{2,1,0:T(2,128)} reshape(f32[256,3072]{1,0:T(8,128)} %add.261) | data formatting | bytes 6291456 | tf_op jit(solution)/shard_map/add | solution.py:68
  378.5 7.3 %multiply_reduce_fusion = bf16[128,3072]{1,0:T(8,128)(2,1)} fusion(f32[128,2,3072]{2,1,0:T(2,128)} %add.262, f32[128,2]{1,0:T(8,128)S(1)} %copy-done.15), kind=kLoop, calls=%fused_computation.5 | loop fusion | flops 1179648 | bytes 3933184 | tf_op jit(solution)/shard_map/reduce_sum | solution.py:70
  (76 shorter events, 11.4 us)
Async XLA Ops:
  6.5 107.8 %copy-start = (bf16[1,256,3072]{2,1,0:T(8,128)(2,1)S(1)}, bf16[1,256,3072]{2,1,0:T(8,128)(2,1)}, u32[]{:S(2)}) copy-start(bf16[1,256,3072]{2,1,0:T(8,128)(2,1)} %param.9) | copy-start | bytes 4718596
  6.5 188.4 %reduce-scatter.2.cloned.1.call-start = ((), (), s32[]{:S(2)}) async-start(), calls=%async_computation.3 | async-start | bytes 4177920 | tf_op jit(solution)/shard_map/reduce_scatter | solution.py:58
  19.1 95.2 %copy-start.17 = (bf16[1,3072,256]{2,1,0:T(8,128)(2,1)S(1)}, bf16[1,3072,256]{2,1,0:T(8,128)(2,1)}, u32[]{:S(2)}) copy-start(bf16[1,3072,256]{2,1,0:T(8,128)(2,1)} %param.8) | copy-start | bytes 4718596
  128.7 141.2 %copy-start.16 = (f32[128,2]{0,1:T(2,128)S(1)}, f32[128,2]{0,1:T(2,128)}, u32[]{:S(2)}) copy-start(f32[128,2]{0,1:T(2,128)} %param.7) | copy-start | bytes 3076
  212.7 10.0 %collective-permute-start = (bf16[8,5,3072]{2,1,0:T(8,128)(2,1)S(1)}, bf16[8,5,3072]{2,1,0:T(8,128)(2,1)S(1)}, u32[]{:S(2)}, u32[]{:S(2)}) collective-permute-start(bf16[8,5,3072]{2,1,0:T(8,128)(2,1)S(1)} %all_to_all.11), channel_id=1, source_target_pairs={{0,1},{1,2},{2,3},{3,4},{4,5},{5,6},{6,7},{7,8},{8,9},{9,10},{10,1... | collective-permute-start | bytes 737288 | tf_op jit(solution)/shard_map/ppermute | solution.py:16
  217.9 7.5 %collective-permute-start.1 = (bf16[8,5,3072]{2,1,0:T(8,128)(2,1)S(1)}, bf16[8,5,3072]{2,1,0:T(8,128)(2,1)S(1)}, u32[]{:S(2)}, u32[]{:S(2)}) collective-permute-start(bf16[8,5,3072]{2,1,0:T(8,128)(2,1)S(1)} %all_to_all.11), channel_id=1, source_target_pairs={{0,15},{1,0},{2,1},{3,2},{4,3},{5,4},{6,5},{7,6},{8,7},{9,8},{10,9... | collective-permute-start | bytes 737288 | tf_op jit(solution)/shard_map/ppermute | solution.py:21
  222.7 7.2 %collective-permute-start.2 = (bf16[8,5,3072]{2,1,0:T(8,128)(2,1)S(1)}, bf16[8,5,3072]{2,1,0:T(8,128)(2,1)S(1)}, u32[]{:S(2)}, u32[]{:S(2)}) collective-permute-start(bf16[8,5,3072]{2,1,0:T(8,128)(2,1)S(1)} %collective-permute-done), channel_id=1, source_target_pairs={{0,1},{1,2},{2,3},{3,4},{4,5},{5,6},{6,7},{7,8},{8,9},{9,10},{10,1... | collective-permute-start | bytes 737288 | tf_op jit(solution)/shard_map/ppermute | solution.py:16
  225.4 7.5 %collective-permute-start.3 = (bf16[8,5,3072]{2,1,0:T(8,128)(2,1)S(1)}, bf16[8,5,3072]{2,1,0:T(8,128)(2,1)S(1)}, u32[]{:S(2)}, u32[]{:S(2)}) collective-permute-start(bf16[8,5,3072]{2,1,0:T(8,128)(2,1)S(1)} %collective-permute-done.1), channel_id=1, source_target_pairs={{0,15},{1,0},{2,1},{3,2},{4,3},{5,4},{6,5},{7,6},{8,7},{9,8},{10,9... | collective-permute-start | bytes 737288 | tf_op jit(solution)/shard_map/ppermute | solution.py:21
  229.9 7.2 %collective-permute-start.4 = (bf16[8,5,3072]{2,1,0:T(8,128)(2,1)S(1)}, bf16[8,5,3072]{2,1,0:T(8,128)(2,1)S(1)}, u32[]{:S(2)}, u32[]{:S(2)}) collective-permute-start(bf16[8,5,3072]{2,1,0:T(8,128)(2,1)S(1)} %collective-permute-done.2), channel_id=1, source_target_pairs={{0,1},{1,2},{2,3},{3,4},{4,5},{5,6},{6,7},{7,8},{8,9},{9,10},{10,1... | collective-permute-start | bytes 737288 | tf_op jit(solution)/shard_map/ppermute | solution.py:16
  232.9 7.5 %collective-permute-start.5 = (bf16[8,5,3072]{2,1,0:T(8,128)(2,1)S(1)}, bf16[8,5,3072]{2,1,0:T(8,128)(2,1)S(1)}, u32[]{:S(2)}, u32[]{:S(2)}) collective-permute-start(bf16[8,5,3072]{2,1,0:T(8,128)(2,1)S(1)} %collective-permute-done.3), channel_id=1, source_target_pairs={{0,15},{1,0},{2,1},{3,2},{4,3},{5,4},{6,5},{7,6},{8,7},{9,8},{10,9... | collective-permute-start | bytes 737288 | tf_op jit(solution)/shard_map/ppermute | solution.py:21
  237.1 3.4 copy-start.1
  237.1 7.4 %collective-permute-start.6 = (bf16[8,5,3072]{2,1,0:T(8,128)(2,1)S(1)}, bf16[8,5,3072]{2,1,0:T(8,128)(2,1)S(1)}, u32[]{:S(2)}, u32[]{:S(2)}) collective-permute-start(bf16[8,5,3072]{2,1,0:T(8,128)(2,1)S(1)} %collective-permute-done.4), channel_id=1, source_target_pairs={{0,1},{1,2},{2,3},{3,4},{4,5},{5,6},{6,7},{7,8},{8,9},{9,10},{10,1... | collective-permute-start | bytes 737288 | tf_op jit(solution)/shard_map/ppermute | solution.py:16
  240.4 4.1 %copy-start.3 = (bf16[8,5,3072]{2,1,0:T(8,128)(2,1)}, bf16[8,5,3072]{2,1,0:T(8,128)(2,1)S(1)}, u32[]{:S(2)}) copy-start(bf16[8,5,3072]{2,1,0:T(8,128)(2,1)S(1)} %collective-permute-done.5) | copy-start | bytes 737284
  240.4 7.5 %collective-permute-start.7 = (bf16[8,5,3072]{2,1,0:T(8,128)(2,1)S(1)}, bf16[8,5,3072]{2,1,0:T(8,128)(2,1)S(1)}, u32[]{:S(2)}, u32[]{:S(2)}) collective-permute-start(bf16[8,5,3072]{2,1,0:T(8,128)(2,1)S(1)} %collective-permute-done.5), channel_id=1, source_target_pairs={{0,15},{1,0},{2,1},{3,2},{4,3},{5,4},{6,5},{7,6},{8,7},{9,8},{10,9... | collective-permute-start | bytes 737288 | tf_op jit(solution)/shard_map/ppermute | solution.py:21
  244.5 3.4 copy-start.5
  244.5 8.4 %collective-permute-start.8 = (bf16[8,5,3072]{2,1,0:T(8,128)(2,1)S(1)}, bf16[8,5,3072]{2,1,0:T(8,128)(2,1)S(1)}, u32[]{:S(2)}, u32[]{:S(2)}) collective-permute-start(bf16[8,5,3072]{2,1,0:T(8,128)(2,1)S(1)} %collective-permute-done.6), channel_id=1, source_target_pairs={{0,1},{1,2},{2,3},{3,4},{4,5},{5,6},{6,7},{7,8},{8,9},{9,10},{10,1... | collective-permute-start | bytes 737288 | tf_op jit(solution)/shard_map/ppermute | solution.py:16
  247.9 5.0 %copy-start.7 = (bf16[8,5,3072]{2,1,0:T(8,128)(2,1)}, bf16[8,5,3072]{2,1,0:T(8,128)(2,1)S(1)}, u32[]{:S(2)}) copy-start(bf16[8,5,3072]{2,1,0:T(8,128)(2,1)S(1)} %collective-permute-done.7) | copy-start | bytes 737284
  247.9 7.2 %collective-permute-start.9 = (bf16[8,5,3072]{2,1,0:T(8,128)(2,1)S(1)}, bf16[8,5,3072]{2,1,0:T(8,128)(2,1)S(1)}, u32[]{:S(2)}, u32[]{:S(2)}) collective-permute-start(bf16[8,5,3072]{2,1,0:T(8,128)(2,1)S(1)} %collective-permute-done.7), channel_id=1, source_target_pairs={{0,15},{1,0},{2,1},{3,2},{4,3},{5,4},{6,5},{7,6},{8,7},{9,8},{10,9... | collective-permute-start | bytes 737288 | tf_op jit(solution)/shard_map/ppermute | solution.py:21
  252.9 2.2 copy-start.9
  252.9 8.4 %collective-permute-start.10 = (bf16[8,5,3072]{2,1,0:T(8,128)(2,1)S(1)}, bf16[8,5,3072]{2,1,0:T(8,128)(2,1)S(1)}, u32[]{:S(2)}, u32[]{:S(2)}) collective-permute-start(bf16[8,5,3072]{2,1,0:T(8,128)(2,1)S(1)} %collective-permute-done.8), channel_id=1, source_target_pairs={{0,1},{1,2},{2,3},{3,4},{4,5},{5,6},{6,7},{7,8},{8,9},{9,10},{10,1... | collective-permute-start | bytes 737288 | tf_op jit(solution)/shard_map/ppermute | solution.py:16
  255.1 6.2 %copy-start.11 = (bf16[8,5,3072]{2,1,0:T(8,128)(2,1)}, bf16[8,5,3072]{2,1,0:T(8,128)(2,1)S(1)}, u32[]{:S(2)}) copy-start(bf16[8,5,3072]{2,1,0:T(8,128)(2,1)S(1)} %collective-permute-done.9) | copy-start | bytes 737284
  255.2 7.3 %collective-permute-start.11 = (bf16[8,5,3072]{2,1,0:T(8,128)(2,1)S(1)}, bf16[8,5,3072]{2,1,0:T(8,128)(2,1)}, u32[]{:S(2)}, u32[]{:S(2)}) collective-permute-start(bf16[8,5,3072]{2,1,0:T(8,128)(2,1)S(1)} %collective-permute-done.9), channel_id=1, source_target_pairs={{0,15},{1,0},{2,1},{3,2},{4,3},{5,4},{6,5},{7,6},{8,7},{9,8},{10,9... | collective-permute-start | bytes 737288 | tf_op jit(solution)/shard_map/ppermute | solution.py:21
  261.3 1.1 copy-start.13
  261.3 8.5 %collective-permute-start.12 = (bf16[8,5,3072]{2,1,0:T(8,128)(2,1)S(1)}, bf16[8,5,3072]{2,1,0:T(8,128)(2,1)}, u32[]{:S(2)}, u32[]{:S(2)}) collective-permute-start(bf16[8,5,3072]{2,1,0:T(8,128)(2,1)S(1)} %collective-permute-done.10), channel_id=1, source_target_pairs={{0,1},{1,2},{2,3},{3,4},{4,5},{5,6},{6,7},{7,8},{8,9},{9,10},{10,1... | collective-permute-start | bytes 737288 | tf_op jit(solution)/shard_map/ppermute | solution.py:16
  262.5 74.1 %collective-permute-start.13 = (bf16[8,5,3072]{2,1,0:T(8,128)(2,1)}, bf16[8,5,3072]{2,1,0:T(8,128)(2,1)}, u32[]{:S(2)}, u32[]{:S(2)}) collective-permute-start(bf16[8,5,3072]{2,1,0:T(8,128)(2,1)} %collective-permute-done.11), channel_id=1, source_target_pairs={{0,15},{1,0},{2,1},{3,2},{4,3},{5,4},{6,5},{7,6},{8,7},{9,8},{10,9... | collective-permute-start | bytes 737288 | tf_op jit(solution)/shard_map/ppermute | solution.py:21
  269.9 71.4 %collective-permute-start.14 = (bf16[8,5,3072]{2,1,0:T(8,128)(2,1)}, bf16[8,5,3072]{2,1,0:T(8,128)(2,1)}, u32[]{:S(2)}, u32[]{:S(2)}) collective-permute-start(bf16[8,5,3072]{2,1,0:T(8,128)(2,1)} %collective-permute-done.12), channel_id=1, source_target_pairs={{0,1},{1,2},{2,3},{3,4},{4,5},{5,6},{6,7},{7,8},{8,9},{9,10},{10,1... | collective-permute-start | bytes 737288 | tf_op jit(solution)/shard_map/ppermute | solution.py:16
  277.6 17.6 %copy-start.2 = (bf16[8,5,3072]{2,1,0:T(8,128)(2,1)S(1)}, bf16[8,5,3072]{2,1,0:T(8,128)(2,1)}, u32[]{:S(2)}) copy-start(bf16[8,5,3072]{2,1,0:T(8,128)(2,1)} %copy-done.1) | copy-start | bytes 737284
  282.1 17.7 %copy-start.4 = (bf16[8,5,3072]{2,1,0:T(8,128)(2,1)S(1)}, bf16[8,5,3072]{2,1,0:T(8,128)(2,1)}, u32[]{:S(2)}) copy-start(bf16[8,5,3072]{2,1,0:T(8,128)(2,1)} %copy-done.3) | copy-start | bytes 737284
  286.7 17.7 %copy-start.6 = (bf16[8,5,3072]{2,1,0:T(8,128)(2,1)S(1)}, bf16[8,5,3072]{2,1,0:T(8,128)(2,1)}, u32[]{:S(2)}) copy-start(bf16[8,5,3072]{2,1,0:T(8,128)(2,1)} %copy-done.5) | copy-start | bytes 737284
  290.6 18.3 %copy-start.8 = (bf16[8,5,3072]{2,1,0:T(8,128)(2,1)S(1)}, bf16[8,5,3072]{2,1,0:T(8,128)(2,1)}, u32[]{:S(2)}) copy-start(bf16[8,5,3072]{2,1,0:T(8,128)(2,1)} %copy-done.7) | copy-start | bytes 737284
  295.2 18.2 %copy-start.10 = (bf16[8,5,3072]{2,1,0:T(8,128)(2,1)S(1)}, bf16[8,5,3072]{2,1,0:T(8,128)(2,1)}, u32[]{:S(2)}) copy-start(bf16[8,5,3072]{2,1,0:T(8,128)(2,1)} %copy-done.9) | copy-start | bytes 737284
  299.8 18.2 %copy-start.12 = (bf16[8,5,3072]{2,1,0:T(8,128)(2,1)S(1)}, bf16[8,5,3072]{2,1,0:T(8,128)(2,1)}, u32[]{:S(2)}) copy-start(bf16[8,5,3072]{2,1,0:T(8,128)(2,1)} %copy-done.11) | copy-start | bytes 737284
  304.4 18.1 %copy-start.14 = (bf16[8,5,3072]{2,1,0:T(8,128)(2,1)S(1)}, bf16[8,5,3072]{2,1,0:T(8,128)(2,1)}, u32[]{:S(2)}) copy-start(bf16[8,5,3072]{2,1,0:T(8,128)(2,1)} %copy-done.13) | copy-start | bytes 737284
  373.4 5.1 %copy-start.15 = (f32[128,2]{1,0:T(8,128)S(1)}, f32[128,2]{1,0:T(8,128)}, u32[]{:S(2)}) copy-start(f32[128,2]{1,0:T(8,128)} %copy.51) | copy-start | bytes 3076
Sparse Core Ops, SparseCore 0:
  128.8 66.0 reduce-scatter.1
